TPU v7x, 256 devices: a whole 4x4x8 slice. The times are simulated.
256 devices in a mesh: row: 4 (over y_lo, core), col: 64 (over x, y_hi, z).
Axes of the slice: x: 4, y: 4 (y_hi: 2, y_lo: 2; y = y_hi * 2 + y_lo), z: 8, core: 2. Of those that a mesh axis runs over, the one named last changes fastest.
Arguments:
- tensor: bfloat16 [128, 3072, 4096], P(None, 'col', 'row'), may hold values from -6 to 6
- first_factor: bfloat16 [64, 4096], P(None, ('row', 'col')), may hold values from -0.453125 to 0.453125
- second_factor: bfloat16 [64, 3072], P(None, 'col'), may hold values from -0.5232237 to 0.5232237
Outputs:
- frames: float32 [64, 128], replicated
- mode_one: float32 [64, 4096], P(None, ('row', 'col'))
All inputs are finite; a program needn't handle non-finite values.
Results may differ from a plain program's by a relative error of at most 0.004.
Values may be sent and summed in bfloat16 or wider, within the bound.
A program may use at most 128 MiB of HBM per device.

v0:
```python
import jax
import jax.numpy as jnp
from jax import lax
from jax.sharding import PartitionSpec as P

ridge_weight = 0.05


def ridge_solve(gram, right_side):
    order_size = gram.shape[0]
    factor_low = jnp.linalg.cholesky(gram + ridge_weight * jnp.eye(order_size, dtype=jnp.float32))
    middle = lax.linalg.triangular_solve(factor_low, right_side, left_side=True, lower=True)
    return lax.linalg.triangular_solve(
        factor_low, middle, left_side=True, lower=True, transpose_a=True
    )


def gram_of(factor):
    return jnp.dot(factor, factor.T, preferred_element_type=jnp.float32)


def spread_product(frames, second):
    product = frames[:, :, None] * second[:, None, :]
    return product.astype(jnp.bfloat16).reshape(frames.shape[0], -1)


def project_columns(flattened, portion):
    return lax.dot_general(
        portion, flattened, (((1,), (1,)), ((), ())), preferred_element_type=jnp.float32
    )


def local(tensor, first_factor, second_factor):
    frame_count, col_count, row_count = tensor.shape
    components = first_factor.shape[0]
    flattened = tensor.reshape(frame_count * col_count, row_count)
    second_values = second_factor.astype(jnp.float32)
    share_rows = row_count // lax.axis_size("col")
    gram_first = lax.psum(gram_of(first_factor), ("row", "col"))
    gram_second = lax.psum(gram_of(second_factor), "col")
    projected = project_columns(flattened, lax.all_gather(first_factor, "col", axis=1, tiled=True))
    projected = projected.reshape(components, frame_count, col_count)
    frame_part = jnp.einsum("rkj,rj->rk", projected, second_values, precision=lax.Precision.HIGHEST)
    frame_sum = lax.psum(frame_part, ("row", "col"))
    frames = ridge_solve(gram_first * gram_second, frame_sum)
    gram_frames = jnp.dot(frames, frames.T, precision=lax.Precision.HIGHEST)
    weights = spread_product(frames, second_values)
    full_part = lax.dot_general(
        weights, flattened, (((1,), (0,)), ((), ())), preferred_element_type=jnp.float32
    )
    first_sum = lax.psum(full_part, "col")
    new_first = ridge_solve(gram_second * gram_frames, first_sum).astype(jnp.bfloat16)
    gram_new = lax.psum(gram_of(new_first), "row")
    projected_new = lax.dot_general(
        new_first, flattened, (((1,), (1,)), ((), ())), preferred_element_type=jnp.float32
    )
    projected_new = projected_new.reshape(components, frame_count, col_count)
    second_part = jnp.einsum("rkj,rk->rj", projected_new, frames, precision=lax.Precision.HIGHEST)
    second_sum = lax.psum(second_part, "row")
    new_second = ridge_solve(gram_new * gram_frames, second_sum)
    weights_next = spread_product(frames, new_second)
    full_next = lax.dot_general(
        weights_next, flattened, (((1,), (0,)), ((), ())), preferred_element_type=jnp.float32
    )
    summed = lax.psum(full_next, "col")
    mode_one = lax.dynamic_slice_in_dim(summed, lax.axis_index("col") * share_rows, share_rows, 1)
    return (frames, mode_one)


def solution(mesh):
    return jax.shard_map(
        local,
        mesh=mesh,
        in_specs=(P(None, "col", "row"), P(None, ("row", "col")), P(None, "col")),
        out_specs=(P(), P(None, ("row", "col"))),
        check_vma=False,
    )
```

profile of v0, /device:TPU:8, one launch (start us, length us, event | category | flops | bytes accessed | tf_op | source)
XLA Modules:
  0.0 2033.9 jit_solution(1604844099440439791)
XLA Ops:
  7.2 185.3 %all_gather.3 = bf16[64,1024]{0,1:T(8,128)(2,1)S(1)} all-gather(bf16[64,16]{0,1:T(8,128)(2,1)} %param.5), channel_id=1, replica_groups=mesh['row'=4,'col'=64] {'col'}, dimensions={1}, use_global_device_ids=true | all-gather | bytes 133120 | tf_op jit(solution)/shard_map/all_gather | solution.py:41
  192.5 0.9 fusion.29
  193.4 1.0 fusion.30
  194.4 0.7 convert_element_type.15
  195.1 17.8 copy.28
  213.0 350.9 %psum.50 = f32[64,64]{1,0:T(8,128)S(1)} all-reduce(f32[64,64]{1,0:T(8,128)S(1)} %fusion.30), channel_id=1, replica_groups=mesh['row'=4,'col'=64] {'col'}, use_global_device_ids=true, to_apply=%region_1.0 | all-reduce | flops 4096 | bytes 32768 | tf_op jit(solution)/shard_map/psum | solution.py:40
  563.9 6.9 fusion.8
  570.8 1.7 fusion.2
  572.5 72.5 %all-reduce = (f32[64,128]{1,0:T(8,128)S(1)}, f32[64,64]{1,0:T(8,128)S(1)}) all-reduce(f32[64,128]{1,0:T(8,128)S(1)} %bitcast.73, f32[64,64]{1,0:T(8,128)S(1)} %fusion.29), channel_id=1, replica_groups=mesh['row'=4,'col'=64] {'row','col'}, use_global_device_ids=true, to_apply=%region_4.0 | all-reduce | flops 12288 | bytes 98304 | tf_op jit(solution)/shard_map/psum | solution.py:44
  645.2 5.9 cholesky.59
  652.4 4.9 custom-call.17
  657.7 7.6 convolution_bitcast_fusion.1
  665.9 5.9 cholesky.70
  673.1 4.9 custom-call.18
  678.0 619.7 %all-reduce.5.cloned.1.call-done = f32[64,1024]{1,0:T(8,128)} async-done(((f32[64,1024]{1,0:T(8,128)}), f32[64,1024]{1,0:T(8,128)}) %all-reduce.5.cloned.1.call-update) | async-done | bytes 262160 | tf_op jit(solution)/shard_map/psum | solution.py:51
  1297.7 1.4 fusion.21
  1299.4 6.9 fusion.10
  1306.5 3.3 fusion
  1309.8 10.7 all-reduce.1
  1320.7 5.9 cholesky.81
  1327.9 4.9 custom-call.19
  1333.2 7.3 convolution_bitcast_fusion
  1340.6 685.2 %all-reduce.7.cloned.1.call-done = f32[64,1024]{0,1:T(8,128)} async-done(((f32[64,1024]{0,1:T(8,128)}), f32[64,1024]{0,1:T(8,128)}) %all-reduce.7.cloned.1.call-update) | async-done | bytes 262160 | tf_op jit(solution)/shard_map/psum | solution.py:65
  2025.8 1.3 constant_dynamic-slice_fusion
  (36 shorter events, 6.4 us)
Async XLA Ops:
  7.2 1290.5 %all-reduce.5.cloned.1.call-start = ((), (), s32[]{:S(2)}) async-start(), calls=%async_computation | async-start | bytes 524288 | tf_op jit(solution)/shard_map/psum | solution.py:51
  195.1 17.8 copy-start.1
  657.7 675.5 %copy-start = (f32[64,128]{1,0:T(8,128)}, f32[64,128]{1,0:T(8,128)S(1)}, u32[]{:S(2)}) copy-start(f32[64,128]{1,0:T(8,128)S(1)} %fusion.24) | copy-start | bytes 98308
  665.3 1360.5 %all-reduce.7.cloned.1.call-start = ((), (), s32[]{:S(2)}) async-start(), calls=%async_computation.1 | async-start | bytes 1048576 | tf_op jit(solution)/shard_map/psum | solution.py:65
Sparse Core Ops, SparseCore 0:
  665.4 632.2 all-reduce.4
  1340.7 685.0 all-reduce.6
where the time goes:
time: 2030 us
  waiting for transfers between devices  1300 us (64%)
  blocking collectives  619 us (30%)
  matrix products  38.5 us (2%)
  other arithmetic  37 us (2%)
    psum x1, waiting for transfers between devices, local(): summed = lax.psum(full_next, 'col')  685 us
    psum x1, waiting for transfers between devices, local(): first_sum = lax.psum(full_part, 'col')  620 us
    psum x1, blocking collectives, local(): gram_second = lax.psum(gram_of(second_factor), 'col')  351 us
    all_gather x1, blocking collectives, local(): lax.all_gather(first_factor, 'col', axis=1, tiled=True)  185 us
    psum x1, blocking collectives, local(): frame_sum = lax.psum(frame_part, ('row', 'col'))  72.5 us
  transfers between devices with their start and end apart: 2, of which 2 were waited for; matrix products, arithmetic and copies ran while one was open for 1% of the time, Pallas kernels for 0%

commit v1 on v0

--- a/solution.py
+++ b/solution.py
@@ -38,7 +38,12 @@
     share_rows = row_count // lax.axis_size("col")
     gram_first = lax.psum(gram_of(first_factor), ("row", "col"))
     gram_second = lax.psum(gram_of(second_factor), "col")
-    projected = project_columns(flattened, lax.all_gather(first_factor, "col", axis=1, tiled=True))
+    projected = project_columns(
+        flattened,
+        jnp.concatenate(
+            lax.all_to_all(jnp.stack([first_factor] * lax.axis_size("col")), "col", 0, 0), axis=1
+        ),
+    )
     projected = projected.reshape(components, frame_count, col_count)
     frame_part = jnp.einsum("rkj,rj->rk", projected, second_values, precision=lax.Precision.HIGHEST)
     frame_sum = lax.psum(frame_part, ("row", "col"))

time: 2030 us -> 1880 us (0.926)
  blocking collectives: 619 us -> 442 us
    all_gather x1 -> x0, blocking collectives: 185 us -> none  [local(): lax.all_gather(first_factor, 'col', axis=1, tiled=True)]
  transfers between devices with their start and end apart: 2 -> 3, of which waited for: 2 -> 2; matrix products, arithmetic and copies ran while one was open for 1% -> 1% of each run, Pallas kernels for 0% -> 0%
where the time goes in v1:
time: 1880 us
  waiting for transfers between devices  1310 us (70%)
  blocking collectives  442 us (24%)
  matrix products  37.7 us (2%)
  other arithmetic  37 us (2%)
  local copies, waits for them, and re-layouts  21.5 us (1%)
    psum x1, waiting for transfers between devices, local(): summed = lax.psum(full_next, 'col')  685 us
    psum x1, waiting for transfers between devices, local(): first_sum = lax.psum(full_part, 'col')  626 us
    psum x1, blocking collectives, local(): gram_second = lax.psum(gram_of(second_factor), 'col')  358 us
    psum x1, blocking collectives, local(): frame_sum = lax.psum(frame_part, ('row', 'col'))  72.5 us
  transfers between devices with their start and end apart: 3, of which 2 were waited for; matrix products, arithmetic and copies ran while one was open for 1% of the time, Pallas kernels for 0%

profile of v1, /device:TPU:8, one launch (start us, length us, event | category | flops | bytes accessed | tf_op | source)
XLA Modules:
  0.0 1876.9 jit_solution(18435310721203412004)
XLA Ops:
  7.9 0.9 reshape.54
  8.7 13.7 all-to-all-start
  22.5 1.0 fusion.28
  23.4 0.7 convert_element_type.15
  24.1 17.8 copy.30
  42.1 358.4 %psum.50 = f32[64,64]{1,0:T(8,128)S(1)} all-reduce(f32[64,64]{1,0:T(8,128)S(1)} %fusion.28), channel_id=1, replica_groups=mesh['row'=4,'col'=64] {'col'}, use_global_device_ids=true, to_apply=%region_1.0 | all-reduce | flops 4096 | bytes 32768 | tf_op jit(solution)/shard_map/psum | solution.py:40
  400.9 6.9 fusion.29
  407.8 1.7 fusion.2
  409.6 72.5 %all-reduce = (f32[64,128]{1,0:T(8,128)S(1)}, f32[64,64]{1,0:T(8,128)S(1)}) all-reduce(f32[64,128]{1,0:T(8,128)S(1)} %bitcast.80, f32[64,64]{1,0:T(8,128)S(1)} %fusion.27), channel_id=1, replica_groups=mesh['row'=4,'col'=64] {'row','col'}, use_global_device_ids=true, to_apply=%region_4.0 | all-reduce | flops 12288 | bytes 98304 | tf_op jit(solution)/shard_map/psum | solution.py:49
  482.2 5.9 cholesky.59
  489.4 4.9 custom-call.17
  495.1 5.9 cholesky.70
  501.0 7.6 convolution_bitcast_fusion.1
  510.1 4.9 custom-call.18
  515.0 625.9 %all-reduce.5.cloned.1.call-done = f32[64,1024]{1,0:T(8,128)} async-done(((f32[64,1024]{1,0:T(8,128)}), f32[64,1024]{1,0:T(8,128)}) %all-reduce.5.cloned.1.call-update) | async-done | bytes 262160 | tf_op jit(solution)/shard_map/psum | solution.py:56
  1140.9 1.4 fusion.19
  1142.6 6.9 fusion.8
  1149.7 3.3 fusion
  1153.0 10.7 all-reduce.1
  1163.9 5.9 cholesky.81
  1171.1 4.9 custom-call.19
  1176.5 7.3 convolution_bitcast_fusion
  1183.8 684.9 %all-reduce.7.cloned.1.call-done = f32[64,1024]{0,1:T(8,128)} async-done(((f32[64,1024]{0,1:T(8,128)}), f32[64,1024]{0,1:T(8,128)}) %all-reduce.7.cloned.1.call-update) | async-done | bytes 262160 | tf_op jit(solution)/shard_map/psum | solution.py:70
  1868.7 1.3 constant_dynamic-slice_fusion
  (42 shorter events, 7.5 us)
Async XLA Ops:
  7.2 0.7 copy-start
  8.7 392.0 %all-to-all-start = ((bf16[64,2,512]{2,1,0:T(2,128)(2,1)}), bf16[64,2,512]{2,1,0:T(2,128)(2,1)S(1)}, u32[]{:S(2)}, u32[]{:S(2)}) async-start(bf16[64,2,512]{2,1,0:T(2,128)(2,1)} %reshape.54), calls=%async_computation | async-start | bytes 262144 | tf_op jit(solution)/shard_map/all_to_all | solution.py:44
  22.4 1118.5 %all-reduce.5.cloned.1.call-start = ((), (), s32[]{:S(2)}) async-start(), calls=%async_computation.1 | async-start | bytes 524288 | tf_op jit(solution)/shard_map/psum | solution.py:56
  24.1 17.8 copy-start.2
  494.7 681.7 %copy-start.1 = (f32[64,128]{1,0:T(8,128)}, f32[64,128]{1,0:T(8,128)S(1)}, u32[]{:S(2)}) copy-start(f32[64,128]{1,0:T(8,128)S(1)} %fusion.22) | copy-start | bytes 98308
  508.6 1360.2 %all-reduce.7.cloned.1.call-start = ((), (), s32[]{:S(2)}) async-start(), calls=%async_computation.2 | async-start | bytes 1048576 | tf_op jit(solution)/shard_map/psum | solution.py:70
Sparse Core Ops, SparseCore 0:
  508.7 632.1 all-reduce.4
  1183.9 684.7 all-reduce.6

commit v2 on v0

--- a/solution.py
+++ b/solution.py
@@ -41,7 +41,7 @@
     projected = project_columns(flattened, lax.all_gather(first_factor, "col", axis=1, tiled=True))
     projected = projected.reshape(components, frame_count, col_count)
     frame_part = jnp.einsum("rkj,rj->rk", projected, second_values, precision=lax.Precision.HIGHEST)
-    frame_sum = lax.psum(frame_part, ("row", "col"))
+    frame_sum = lax.psum(lax.psum(frame_part, "row"), "col")
     frames = ridge_solve(gram_first * gram_second, frame_sum)
     gram_frames = jnp.dot(frames, frames.T, precision=lax.Precision.HIGHEST)
     weights = spread_product(frames, second_values)

time: 2030 us -> 2040 us (level)
    psum x2 -> x3, blocking collectives: 423 us -> 437 us  [the longest x2 364 us: local(): frame_sum = lax.psum(lax.psum(frame_part, 'row'), 'col')]
where the time goes in v2:
time: 2040 us
  waiting for transfers between devices  1300 us (64%)
  blocking collectives  633 us (31%)
  matrix products  38.5 us (2%)
  other arithmetic  37 us (2%)
    psum x1, waiting for transfers between devices, local(): summed = lax.psum(full_next, 'col')  685 us
    psum x1, waiting for transfers between devices, local(): first_sum = lax.psum(full_part, 'col')  616 us
    psum x2, blocking collectives, local(): frame_sum = lax.psum(lax.psum(frame_part, 'row'), 'col')  364 us
    all_gather x1, blocking collectives, local(): lax.all_gather(first_factor, 'col', axis=1, tiled=True)  185 us
    psum x1, blocking collectives, local(): gram_first = lax.psum(gram_of(first_factor), ('row', 'col'))  72.5 us
  transfers between devices with their start and end apart: 2, of which 2 were waited for; matrix products, arithmetic and copies ran while one was open for 1% of the time, Pallas kernels for 0%

profile of v2, /device:TPU:8, one launch (start us, length us, event | category | flops | bytes accessed | tf_op | source)
XLA Modules:
  0.0 2043.6 jit_solution(8261557259844210761)
XLA Ops:
  7.2 185.3 %all_gather.3 = bf16[64,1024]{0,1:T(8,128)(2,1)S(1)} all-gather(bf16[64,16]{0,1:T(8,128)(2,1)} %param.5), channel_id=1, replica_groups=mesh['row'=4,'col'=64] {'col'}, dimensions={1}, use_global_device_ids=true | all-gather | bytes 133120 | tf_op jit(solution)/shard_map/all_gather | solution.py:41
  192.5 0.9 fusion.29
  193.4 1.0 fusion.30
  195.1 17.8 copy.28
  213.0 6.9 fusion.8
  219.9 1.7 fusion.2
  221.7 10.3 psum.58
  231.9 72.5 %psum.56 = f32[64,64]{1,0:T(8,128)S(1)} all-reduce(f32[64,64]{1,0:T(8,128)S(1)} %fusion.29), channel_id=1, replica_groups=mesh['row'=4,'col'=64] {'row','col'}, use_global_device_ids=true, to_apply=%region_0.0 | all-reduce | flops 4096 | bytes 32768 | tf_op jit(solution)/shard_map/psum | solution.py:39
  304.4 353.9 %all-reduce = (f32[64,128]{1,0:T(8,128)S(1)}, f32[64,64]{1,0:T(8,128)S(1)}) all-reduce(f32[64,128]{1,0:T(8,128)S(1)} %psum.58, f32[64,64]{1,0:T(8,128)S(1)} %fusion.30), channel_id=1, replica_groups=mesh['row'=4,'col'=64] {'col'}, use_global_device_ids=true, to_apply=%region_5.0 | all-reduce | flops 12288 | bytes 98304 | tf_op jit(solution)/shard_map/psum | solution.py:44
  658.5 5.9 cholesky.59
  665.7 4.9 custom-call.17
  671.0 7.6 convolution_bitcast_fusion.1
  679.2 5.9 cholesky.70
  686.4 4.9 custom-call.18
  691.3 616.3 %all-reduce.5.cloned.1.call-done = f32[64,1024]{1,0:T(8,128)} async-done(((f32[64,1024]{1,0:T(8,128)}), f32[64,1024]{1,0:T(8,128)}) %all-reduce.5.cloned.1.call-update) | async-done | bytes 262160 | tf_op jit(solution)/shard_map/psum | solution.py:51
  1307.6 1.4 fusion.21
  1309.3 6.9 fusion.10
  1316.4 3.3 fusion
  1319.7 10.7 all-reduce.1
  1330.6 5.9 cholesky.81
  1337.8 4.9 custom-call.19
  1343.1 7.3 convolution_bitcast_fusion
  1350.5 684.9 %all-reduce.7.cloned.1.call-done = f32[64,1024]{0,1:T(8,128)} async-done(((f32[64,1024]{0,1:T(8,128)}), f32[64,1024]{0,1:T(8,128)}) %all-reduce.7.cloned.1.call-update) | async-done | bytes 262160 | tf_op jit(solution)/shard_map/psum | solution.py:65
  2035.4 1.3 constant_dynamic-slice_fusion
  (37 shorter events, 7.1 us)
Async XLA Ops:
  7.2 1300.4 %all-reduce.5.cloned.1.call-start = ((), (), s32[]{:S(2)}) async-start(), calls=%async_computation | async-start | bytes 524288 | tf_op jit(solution)/shard_map/psum | solution.py:51
  195.1 17.8 copy-start.1
  671.0 672.1 %copy-start = (f32[64,128]{1,0:T(8,128)}, f32[64,128]{1,0:T(8,128)S(1)}, u32[]{:S(2)}) copy-start(f32[64,128]{1,0:T(8,128)S(1)} %fusion.24) | copy-start | bytes 98308
  678.6 1356.8 %all-reduce.7.cloned.1.call-start = ((), (), s32[]{:S(2)}) async-start(), calls=%async_computation.1 | async-start | bytes 1048576 | tf_op jit(solution)/shard_map/psum | solution.py:65
Sparse Core Ops, SparseCore 0:
  678.8 628.7 all-reduce.4
  1350.6 684.7 all-reduce.6

commit v3 on v0

--- a/solution.py
+++ b/solution.py
@@ -41,7 +41,7 @@
     projected = project_columns(flattened, lax.all_gather(first_factor, "col", axis=1, tiled=True))
     projected = projected.reshape(components, frame_count, col_count)
     frame_part = jnp.einsum("rkj,rj->rk", projected, second_values, precision=lax.Precision.HIGHEST)
-    frame_sum = lax.psum(frame_part, ("row", "col"))
+    frame_sum = jnp.sum(lax.all_gather(frame_part, ("row", "col")), axis=0)
     frames = ridge_solve(gram_first * gram_second, frame_sum)
     gram_frames = jnp.dot(frames, frames.T, precision=lax.Precision.HIGHEST)
     weights = spread_product(frames, second_values)

time: 2030 us -> 2320 us (1.14)
  waiting for transfers between devices: 1300 us -> 1580 us
    all_gather x0 -> x1, waiting for transfers between devices: none -> 245 us  [local(): frame_sum = jnp.sum(lax.all_gather(frame_part, ('row', 'col')), axis=0)]
    psum x1, waiting for transfers between devices: 620 us -> 651 us  [local(): first_sum = lax.psum(full_part, 'col')]
  transfers between devices with their start and end apart: 2 -> 3, of which waited for: 2 -> 3; matrix products, arithmetic and copies ran while one was open for 1% -> 1% of each run, Pallas kernels for 0% -> 0%
where the time goes in v3:
time: 2320 us
  waiting for transfers between devices  1580 us (68%)
  blocking collectives  621 us (27%)
  other arithmetic  40.2 us (2%)
  matrix products  37.6 us (2%)
    psum x1, waiting for transfers between devices, local(): summed = lax.psum(full_next, 'col')  685 us
    psum x1, waiting for transfers between devices, local(): first_sum = lax.psum(full_part, 'col')  651 us
    psum x1, blocking collectives, local(): gram_second = lax.psum(gram_of(second_factor), 'col')  354 us
    all_gather x1, waiting for transfers between devices, local(): frame_sum = jnp.sum(lax.all_gather(frame_part, ('row', 'col')), axis=0)  245 us
    all_gather x1, blocking collectives, local(): lax.all_gather(first_factor, 'col', axis=1, tiled=True)  185 us
    psum x1, blocking collectives, local(): gram_first = lax.psum(gram_of(first_factor), ('row', 'col'))  72.1 us
  transfers between devices with their start and end apart: 3, of which 3 were waited for; matrix products, arithmetic and copies ran while one was open for 1% of the time, Pallas kernels for 0%

profile of v3, /device:TPU:8, one launch (start us, length us, event | category | flops | bytes accessed | tf_op | source)
XLA Modules:
  0.0 2315.6 jit_solution(5932671018374344517)
XLA Ops:
  7.2 0.8 copy.30
  8.0 17.8 copy.28
  25.9 185.0 %all_gather.9 = bf16[64,1024]{0,1:T(8,128)(2,1)S(1)} all-gather(bf16[64,16]{0,1:T(8,128)(2,1)S(1)} %copy-done.2), channel_id=1, replica_groups=mesh['row'=4,'col'=64] {'col'}, dimensions={1}, use_global_device_ids=true | all-gather | bytes 133120 | tf_op jit(solution)/shard_map/all_gather | solution.py:41
  210.9 6.9 fusion.8
  217.8 2.3 fusion.2
  220.4 72.1 %psum.42 = f32[64,64]{1,0:T(8,128)S(1)} all-reduce(f32[64,64]{1,0:T(8,128)S(1)} %fusion.29), channel_id=1, replica_groups=mesh['row'=4,'col'=64] {'row','col'}, use_global_device_ids=true, to_apply=%region_0.0 | all-reduce | flops 4096 | bytes 32768 | tf_op jit(solution)/shard_map/psum | solution.py:39
  292.7 353.5 %psum.43 = f32[64,64]{1,0:T(8,128)S(1)} all-reduce(f32[64,64]{1,0:T(8,128)S(1)} %fusion.30), channel_id=1, replica_groups=mesh['row'=4,'col'=64] {'col'}, use_global_device_ids=true, to_apply=%region_1.0 | all-reduce | flops 4096 | bytes 32768 | tf_op jit(solution)/shard_map/psum | solution.py:40
  646.4 5.9 cholesky.59
  653.6 4.9 custom-call.17
  658.5 245.2 %all-gather.3.cloned.1.call-done = f32[16384,128]{1,0:T(8,128)} async-done(((f32[64,128]{1,0:T(8,128)}), f32[16384,128]{1,0:T(8,128)}) %all-gather.3.cloned.1.call-update) | async-done | bytes 8388624 | tf_op jit(solution)/shard_map/all_gather | solution.py:44
  903.7 3.9 reduce_sum.9
  908.3 7.6 convolution_bitcast_fusion.1
  916.2 5.9 cholesky.70
  923.4 4.9 custom-call.18
  928.3 651.3 %all-reduce.4.cloned.1.call-done = f32[64,1024]{1,0:T(8,128)} async-done(((f32[64,1024]{1,0:T(8,128)}), f32[64,1024]{1,0:T(8,128)}) %all-reduce.4.cloned.1.call-update) | async-done | bytes 262160 | tf_op jit(solution)/shard_map/psum | solution.py:51
  1579.7 1.4 fusion.21
  1581.4 6.9 fusion.10
  1588.4 3.3 fusion
  1591.8 10.7 all-reduce
  1602.7 5.9 cholesky.81
  1609.9 4.9 custom-call.19
  1615.2 7.3 convolution_bitcast_fusion
  1622.6 685.2 %all-reduce.6.cloned.1.call-done = f32[64,1024]{0,1:T(8,128)} async-done(((f32[64,1024]{0,1:T(8,128)}), f32[64,1024]{0,1:T(8,128)}) %all-reduce.6.cloned.1.call-update) | async-done | bytes 262160 | tf_op jit(solution)/shard_map/psum | solution.py:65
  2307.8 1.3 constant_dynamic-slice_fusion
  (42 shorter events, 6.7 us)
Async XLA Ops:
  7.2 896.6 %all-gather.3.cloned.1.call-start = ((), (), s32[]{:S(2)}) async-start(), calls=%async_computation.2 | async-start | bytes 8421376 | tf_op jit(solution)/shard_map/all_gather | solution.py:44
  8.0 17.8 copy-start.2
  217.8 2.4 copy-start.1
  220.2 1359.5 %all-reduce.4.cloned.1.call-start = ((), (), s32[]{:S(2)}) async-start(), calls=%async_computation | async-start | bytes 524288 | tf_op jit(solution)/shard_map/psum | solution.py:51
  908.1 707.1 %copy-start = (f32[64,128]{1,0:T(8,128)}, f32[64,128]{1,0:T(8,128)S(1)}, u32[]{:S(2)}) copy-start(f32[64,128]{1,0:T(8,128)S(1)} %fusion.24) | copy-start | bytes 98308
  915.8 1391.9 %all-reduce.6.cloned.1.call-start = ((), (), s32[]{:S(2)}) async-start(), calls=%async_computation.1 | async-start | bytes 1048576 | tf_op jit(solution)/shard_map/psum | solution.py:65
Sparse Core Ops, SparseCore 0:
  220.3 683.4 all-gather.2
  916.0 663.6 all-reduce.3
  1622.7 685.0 all-reduce.5
